TPU v7x, 32 devices: a whole 2x2x4 slice. The times are simulated.
32 devices in a mesh: groups: 2 (over x), lon: 16 (over z, y, core).
Axes of the slice: x: 2, y: 2, z: 4, core: 2. Of those that a mesh axis runs over, the one named last changes fastest.
Arguments:
- fields: bfloat16 [128, 512, 256], P('groups', 'lon'), parts along dimension 0, may hold values from -36 to 36
- sea_mask: int32 [128, 512], P('groups', 'lon'), parts along dimension 0, may hold values 0 or 1
- cotangent: bfloat16 [128, 512, 256], P('groups', 'lon'), parts along dimension 0, may hold values from -6 to 6
- depth_kernel: float32 [7, 7, 256], replicated, may hold values from -0.875 to 0.875
- norm_gain: float32 [256], replicated, may hold values from 0.1 to 1.9
- up_weight: bfloat16 [256, 1024], replicated, may hold values from -0.375 to 0.375
- down_weight: bfloat16 [256, 1024], replicated, may hold values from -0.1875 to 0.1875
- layer_scale: float32 [256], replicated, may hold values from 0.3 to 3
Outputs:
- grad_fields: bfloat16 [128, 512, 256], P('groups', 'lon'), parts along dimension 0
- grad_kernel: float32 [14, 7, 256], P('groups'), parts along dimension 0
- grad_up: float32 [256, 2048], P('lon', 'groups'), parts along dimension 1
- grad_down: float32 [256, 2048], P('lon', 'groups'), parts along dimension 1
There are 2 independent parts, one for each index of `groups`. A program takes and returns all parts, laid end to end along the dimension named above; an argument that names none is the same for every part. Nothing has to cross between parts.
All inputs are finite; a program needn't handle non-finite values. No bound on the sum of `sea_mask` on one device may be relied on, other than what follows from the above.
Results may differ from a plain program's by a relative error of at most 0.0063.
Values may be sent and summed in bfloat16 or wider, within the bound.
A program may use at most 128 MiB of HBM per device.

v0:
```python
import math
import jax
import jax.numpy as jnp
from jax import lax
from jax.sharding import PartitionSpec as P


def from_partner(block, axis, bit):
    count = lax.axis_size(axis)
    route = []
    for low in range(count):
        high = low | 1 << bit
        if high != low and high < count:
            route += [(low, high), (high, low)]
    return lax.ppermute(block, axis, route)


def extended_2(cells, sides, width):
    for axis, dim in sides:
        count = lax.axis_size(axis)
        head = lax.slice_in_dim(cells, 0, width, axis=dim)
        tail = lax.slice_in_dim(cells, cells.shape[dim] - width, cells.shape[dim], axis=dim)
        cells = jnp.concatenate(
            [
                lax.ppermute(tail, axis, [(i, (i + 1) % count) for i in range(count)]),
                cells,
                lax.ppermute(head, axis, [((i + 1) % count, i) for i in range(count)]),
            ],
            axis=dim,
        )
    return cells


def gelu_tanh(values):
    return jax.nn.gelu(values, approximate=True)


def local(
    fields, sea_mask, cotangent, depth_kernel, norm_gain, up_weight, down_weight, layer_scale
):
    band_rows, band_cols, channels = fields.shape
    devices = lax.axis_size("lon")
    mask_bf = sea_mask.astype(jnp.bfloat16)[:, :, None]
    masked = fields * mask_bf
    seam_rows = masked[band_rows - 3 :]
    partner_rows = seam_rows
    for bit in range(devices.bit_length() - 1):
        partner_rows = from_partner(partner_rows, "lon", bit)
    ghost = partner_rows[::-1, ::-1]
    south = jnp.zeros((3, band_cols, channels), jnp.bfloat16)
    padded = jnp.concatenate([south, masked, ghost], axis=0)
    extended = extended_2(padded, (("lon", 1),), 3)
    ext_wide = extended.astype(jnp.float32)
    conv = jnp.zeros((band_rows, band_cols, channels), jnp.float32)
    for row_tap in range(7):
        for col_tap in range(7):
            conv = (
                conv
                + depth_kernel[row_tap, col_tap]
                * ext_wide[row_tap : row_tap + band_rows, col_tap : col_tap + band_cols]
            )
    mean_z = jnp.mean(conv, axis=-1, keepdims=True)
    centred = conv - mean_z
    inv_std = lax.rsqrt(jnp.mean(centred * centred, axis=-1, keepdims=True) + 1e-06)
    nhat = centred * inv_std
    cells = band_rows * band_cols
    normed = (nhat * norm_gain).astype(jnp.bfloat16).reshape(cells, channels)
    dout = (
        (cotangent.astype(jnp.float32) * layer_scale * mask_bf.astype(jnp.float32))
        .astype(jnp.bfloat16)
        .reshape(cells, channels)
    )
    preact = jnp.dot(normed, up_weight, preferred_element_type=jnp.float32)
    hidden = gelu_tanh(preact).astype(jnp.bfloat16)
    dhid = jnp.dot(dout, down_weight, preferred_element_type=jnp.float32)
    _, back = jax.vjp(gelu_tanh, preact)
    dpre = back(dhid)[0].astype(jnp.bfloat16)
    contract_rows = (((0,), (0,)), ((), ()))
    contract_cols = (((1,), (1,)), ((), ()))
    factor = 1.0 / math.sqrt(cells * devices)
    hidden_width = up_weight.shape[1]
    term_up = lax.dot_general(normed, dpre, contract_rows, preferred_element_type=jnp.float32)
    term_down = lax.dot_general(dout, hidden, contract_rows, preferred_element_type=jnp.float32)
    owned = lax.psum_scatter(
        jnp.concatenate([term_up, term_down], axis=1) * factor,
        "lon",
        scatter_dimension=0,
        tiled=True,
    )
    grad_up = owned[:, :hidden_width]
    grad_down = owned[:, hidden_width:]
    dnorm = lax.dot_general(dpre, up_weight, contract_cols, preferred_element_type=jnp.float32)
    scaled = dnorm.reshape(band_rows, band_cols, channels) * norm_gain
    grad_conv = inv_std * (
        scaled
        - jnp.mean(scaled, axis=-1, keepdims=True)
        - nhat * jnp.mean(scaled * nhat, axis=-1, keepdims=True)
    )
    taps = []
    for row_tap in range(7):
        for col_tap in range(7):
            taps.append(
                jnp.sum(
                    grad_conv
                    * ext_wide[row_tap : row_tap + band_rows, col_tap : col_tap + band_cols],
                    axis=(0, 1),
                )
            )
    local_kernel = jnp.stack(taps, axis=0).reshape(7, 7, channels) * factor
    grad_kernel = lax.psum(local_kernel, "lon")
    grad_pad = jnp.pad(grad_conv, ((6, 6), (6, 6), (0, 0)))
    grad_ext = jnp.zeros((band_rows + 6, band_cols + 6, channels), jnp.float32)
    for row_tap in range(7):
        for col_tap in range(7):
            grad_ext = (
                grad_ext
                + depth_kernel[row_tap, col_tap]
                * grad_pad[
                    6 - row_tap : 12 - row_tap + band_rows, 6 - col_tap : 12 - col_tap + band_cols
                ]
            )
    rims = jnp.concatenate([grad_ext[:, :3], grad_ext[:, band_cols + 3 :]], axis=1)
    arrived = extended_2(rims.astype(jnp.bfloat16), (("lon", 1),), 3).astype(rims.dtype)
    grad_padded = grad_ext[:, 3 : band_cols + 3]
    grad_padded = grad_padded.at[:, :3].add(arrived[:, :3])
    grad_padded = grad_padded.at[:, band_cols - 3 :].add(arrived[:, 9:])
    seam_grads = grad_padded[band_rows + 3 :]
    partner_grads = seam_grads
    for bit in range(devices.bit_length() - 1):
        partner_grads = from_partner(partner_grads.astype(jnp.bfloat16), "lon", bit).astype(
            partner_grads.dtype
        )
    grad_masked = grad_padded[3 : band_rows + 3]
    grad_masked = grad_masked.at[band_rows - 3 :].add(partner_grads[::-1, ::-1])
    grad_fields = (
        cotangent.astype(jnp.float32) + mask_bf.astype(jnp.float32) * grad_masked
    ).astype(jnp.bfloat16)
    return (grad_fields, grad_kernel, grad_up, grad_down)


def solution(mesh):
    return jax.shard_map(
        local,
        mesh=mesh,
        in_specs=(
            P("groups", "lon", None),
            P("groups", "lon"),
            P("groups", "lon", None),
            P(),
            P(),
            P(),
            P(),
            P(),
        ),
        out_specs=(
            P("groups", "lon", None),
            P("groups", None, None),
            P("lon", "groups"),
            P("lon", "groups"),
        ),
        check_vma=False,
    )
```

profile of v0, /device:TPU:0, one launch (start us, length us, event | category | flops | bytes accessed | tf_op | source)
XLA Modules:
  0.0 221.3 jit_solution(10699872550884711838)
XLA Ops:
  11.2 2.9 %collective-permute-start.1 = (bf16[3,32,256]{2,1,0:T(8,128)(2,1)S(1)}, bf16[3,32,256]{2,1,0:T(8,128)(2,1)S(1)}, u32[]{:S(2)}, u32[]{:S(2)}) collective-permute-start(bf16[3,32,256]{2,1,0:T(8,128)(2,1)S(1)} %collective-permute-done), channel_id=1, source_target_pairs={{0,2},{2,0},{1,3},{3,1},{4,6},{6,4},{5,7},{7,5},{8,10},{10,8},{9,1... | collective-permute-start | bytes 147464 | tf_op jit(solution)/shard_map/ppermute | solution.py:15
  16.1 2.1 collective-permute-start.2
  18.3 2.0 collective-permute-done.2
  20.3 3.0 %collective-permute-start.3 = (bf16[3,32,256]{2,1,0:T(8,128)(2,1)S(1)}, bf16[3,32,256]{2,1,0:T(8,128)(2,1)S(1)}, u32[]{:S(2)}, u32[]{:S(2)}) collective-permute-start(bf16[3,32,256]{2,1,0:T(8,128)(2,1)S(1)} %collective-permute-done.2), channel_id=1, source_target_pairs={{0,8},{8,0},{1,9},{9,1},{2,10},{10,2},{3,11},{11,3},{4,12},{12,4},... | collective-permute-start | bytes 147464 | tf_op jit(solution)/shard_map/ppermute | solution.py:15
  25.6 4.4 %collective-permute-start.5 = (bf16[70,3,256]{2,1,0:T(4,128)(2,1)S(1)}, bf16[70,3,256]{2,1,0:T(4,128)(2,1)S(1)}, u32[]{:S(2)}, u32[]{:S(2)}) collective-permute-start(bf16[70,3,256]{2,1,0:T(4,128)(2,1)S(1)} %get-tuple-element.97), channel_id=1, source_target_pairs={{1,0},{2,1},{3,2},{4,3},{5,4},{6,5},{7,6},{8,7},{9,8},{10,9},{11,1... | collective-permute-start | bytes 322568 | tf_op jit(solution)/shard_map/ppermute | solution.py:27
  30.3 2.7 %collective-permute-done.4 = bf16[70,3,256]{2,1,0:T(4,128)(2,1)S(1)} collective-permute-done((bf16[70,3,256]{2,1,0:T(4,128)(2,1)S(1)}, bf16[70,3,256]{2,1,0:T(4,128)(2,1)S(1)}, u32[]{:S(2)}, u32[]{:S(2)}) %collective-permute-start.4) | collective-permute-done | bytes 107552 | tf_op jit(solution)/shard_map/ppermute | solution.py:25
  35.2 15.9 %fusion.115 = (f32[64,32]{1,0:T(8,128)S(1)}, f32[64,32,256]{2,1,0:T(8,128)}) fusion(f32[70,38,256]{2,1,0:T(8,128)S(1)} %maximum_convert_fusion, f32[256]{0:T(256)S(1)} %bitcast.211, f32[256]{0:T(256)S(1)} %bitcast.213, f32[256]{0:T(256)S(1)} %bitcast.119, f32[256]{0:T(256)S(1)} %bitcast.121, f32[256]{0:T(256)S(1)} %bitcast.123, f32[256]{0:T(256)S(1)} %bitcast.125, ...), kind=kLoop, calls=%fused_computation.242 | loop fusion | flops 51378176 | bytes 104915968 | tf_op jit(solution)/shard_map/reduce_sum | solution.py:62
  51.1 2.4 %multiply_reduce_fusion.51 = f32[64,32]{1,0:T(8,128)S(1)} fusion(f32[64,32,256]{2,1,0:T(8,128)} %get-tuple-element.93, f32[64,32]{1,0:T(8,128)S(1)} %broadcast_multiply_fusion.3), kind=kLoop, calls=%fused_computation.216 | loop fusion | flops 1570816 | bytes 2113536 | tf_op jit(solution)/shard_map/reduce_sum | solution.py:64
  55.9 4.2 %fusion.7 = f32[256,1024]{1,0:T(8,128)} fusion(bf16[2048,256]{1,0:T(8,128)(2,1)S(1)} %bitcast.115, f32[2048,1024]{1,0:T(8,128)S(1)} %fusion.121), kind=kOutput, calls=%fused_computation.59 | convolution fusion | flops 1092616192 | bytes 10485760 | tf_op jit(solution)/shard_map/dot_general | solution.py:83
  60.1 6.3 %fusion.6 = bf16[2048,1024]{1,0:T(8,128)(2,1)S(1)} fusion(f32[2048,1024]{1,0:T(8,128)S(1)} %fusion.121, bf16[2048,256]{1,0:T(8,128)(2,1)S(1)} %bitcast.116, bf16[256,1024]{1,0:T(8,128)(2,1)S(1)} %copy-done.109), kind=kOutput, calls=%fused_computation.57 | convolution fusion | flops 1115684864 | bytes 14155776 | tf_op jit(solution)/shard_map/dot_general | solution.py:75
  66.3 2.6 %multiply_reduce_fusion.50 = (f32[2048]{0:T(1024)S(1)}, f32[2048,256]{1,0:T(8,128)}) fusion(f32[256]{0:T(256)S(1)} %copy-done.17, bf16[2048,1024]{1,0:T(8,128)(2,1)S(1)} %fusion.6, bf16[256,1024]{1,0:T(8,128)(2,1)S(1)} %copy-done), kind=kOutput, calls=%fused_computation.214 | convolution fusion | flops 1074788352 | bytes 6824960 | tf_op jit(solution)/shard_map/dot_general | solution.py:92
  69.1 2.9 %multiply_reduce_fusion.49 = f32[64,32]{1,0:T(8,128)S(1)} fusion(f32[64,32,256]{2,1,0:T(8,128)} %bitcast.112, f32[64,32,256]{2,1,0:T(8,128)} %get-tuple-element.93, f32[256]{0:T(256)S(1)} %copy-done.17, f32[64,32]{1,0:T(8,128)S(1)} %add_rsqrt_fusion, f32[64,32]{1,0:T(8,128)S(1)} %broadcast_multiply_fusion.3), kind=kLoop, calls=%fused_computation.213 | loop fusion | flops 2619392 | bytes 4219904 | tf_op jit(solution)/shard_map/reduce_sum | solution.py:97
  72.9 6.6 %multiply_reduce_fusion = (f32[256]{0:T(256)}, f32[256]{0:T(256)}, f32[256]{0:T(256)}, f32[256]{0:T(256)}, f32[256]{0:T(256)}, /*index=5*/f32[256]{0:T(256)}, f3...) fusion(f32[70,38,256]{2,1,0:T(8,128)S(1)} %maximum_convert_fusi, ...), kind=kLoop, calls=%fused_computation.163 | loop fusion | flops 22539776 | bytes 44092416 | tf_op jit(solution)/shard_map/reduce_sum | solution.py:103
  79.9 22.2 %fusion.113 = (bf16[70,38,256]{2,1,0:T(8,128)(2,1)S(1)}, f32[70,38,256]{2,1,0:T(8,128)S(1)}) fusion(f32[256]{0:T(256)S(1)} %bitcast.212, f32[256]{0:T(256)S(1)} %bitcast.214, f32[256]{0:T(256)S(1)} %bitcast.120, f32[256]{0:T(256)S(1)} %bitcast.122, f32[256]{0:T(256)S(1)} %bitcast.124, f32[256]{0:T(256)S(1)} %bitcast.126, f32[256]{0:T(256)S(1)} %bitcast.128, ...), kind=kLoop, calls=%fused_computation.241 | loop fusion | flops 66734080 | bytes 6233088 | tf_op jit(solution)/shard_map/convert.3
  103.0 3.8 %collective-permute-start.7 = (bf16[70,3,256]{2,1,0:T(4,128)(2,1)S(1)}, bf16[70,3,256]{2,1,0:T(4,128)(2,1)S(1)}, u32[]{:S(2)}, u32[]{:S(2)}) collective-permute-start(bf16[70,3,256]{2,1,0:T(4,128)(2,1)S(1)} %get-tuple-element.95), channel_id=1, source_target_pairs={{1,0},{2,1},{3,2},{4,3},{5,4},{6,5},{7,6},{8,7},{9,8},{10,9},{11,1... | collective-permute-start | bytes 322568 | tf_op jit(solution)/shard_map/ppermute | solution.py:27
  106.8 4.5 %fusion.122 = f32[256,1024]{1,0:T(8,128)} fusion(bf16[2048,256]{1,0:T(8,128)(2,1)S(1)} %bitcast.114, bf16[2048,1024]{1,0:T(8,128)(2,1)} %copy-done.110), kind=kOutput, calls=%fused_computation.249 | convolution fusion | flops 1073741824 | bytes 6291456 | tf_op jit(solution)/shard_map/dot_general | solution.py:82
  115.4 5.2 %scatter-add.10 = f32[70,32,256]{2,1,0:T(8,128)} dynamic-update-slice(f32[70,32,256]{2,1,0:T(8,128)} %slice.866, f32[70,3,256]{2,1,0:T(4,128)} %convert_add_fusion.1, s32[]{:T(128)} %constant.108.clone.1, s32[]{:T(128)} %constant.108.clone.1, s32[]{:T(128)} %constant.108.clone.1) | dynamic-update-slice | bytes 430084 | tf_op jit(solution)/shard_map/scatter-add | solution.py:125
  120.6 2.1 slice_add_fusion
  122.8 4.6 %scatter-add.11 = f32[70,32,256]{2,1,0:T(8,128)} dynamic-update-slice(f32[70,32,256]{2,1,0:T(8,128)} %scatter-add.10, f32[70,3,256]{2,1,0:T(4,128)} %slice_add_fusion, s32[]{:T(128)} %constant.108.clone.1, s32[]{:T(128)} %constant.109.clone.1, s32[]{:T(128)} %constant.108.clone.1) | dynamic-update-slice | bytes 430084 | tf_op jit(solution)/shard_map/scatter-add | solution.py:126
  128.2 3.2 %maximum_multiply_fusion = f32[256,2048]{1,0:T(8,128)} fusion(f32[256,1024]{1,0:T(8,128)} %fusion.7, f32[256,1024]{1,0:T(8,128)} %fusion.122), kind=kLoop, calls=%fused_computation.162 | loop fusion | flops 1048576 | bytes 4194304 | tf_op jit(solution)/shard_map/mul | solution.py:85
  131.5 6.1 %multiply_reduce_fusion.18 = (f32[256]{0:T(256)S(1)}, f32[256]{0:T(256)S(1)}, f32[256]{0:T(256)S(1)}, f32[256]{0:T(256)S(1)}, f32[256]{0:T(256)S(1)}, /*index=5*...) fusion(f32[64,32,256]{2,1,0:T(8,128)} %copy-done.3, ...), kind=kLoop, calls=%fused_computation.181 | loop fusion | flops 18869760 | bytes 39864320 | tf_op jit(solution)/shard_map/reduce_sum | solution.py:103
  138.0 4.3 %multiply_reduce_fusion.36 = (f32[256]{0:T(256)S(1)}, f32[256]{0:T(256)S(1)}, f32[256]{0:T(256)S(1)}, f32[256]{0:T(256)S(1)}, f32[256]{0:T(256)}, /*index=5*/f32...) fusion(f32[64,32,256]{2,1,0:T(8,128)S(1)} %copy-done.4, ...), kind=kLoop, calls=%fused_computation.199 | loop fusion | flops 13628160 | bytes 29373440 | tf_op jit(solution)/shard_map/reduce_sum | solution.py:103
  145.8 61.8 %psum.7 = f32[7,7,256]{2,1,0:T(8,128)} all-reduce(f32[7,7,256]{2,1,0:T(8,128)S(1)} %mul.1497), channel_id=1, replica_groups=mesh['groups'=2,'lon'=16] {'lon'}, use_global_device_ids=true, to_apply=%region_53.0 | all-reduce | flops 12544 | bytes 100352 | tf_op jit(solution)/shard_map/psum | solution.py:110
  210.4 2.5 %fusion.107 = bf16[64,32,256]{2,1,0:T(8,128)(2,1)} fusion(bf16[64,32,256]{2,1,0:T(8,128)(2,1)} %param.16, f32[64,32,256]{2,1,0:T(8,128)S(1)} %fusion.108, f32[64,32]{1,0:T(8,128)S(1)} %copy-done.15), kind=kLoop, calls=%fused_computation.161 | loop fusion | flops 2097152 | bytes 4202496 | tf_op jit(solution)/shard_map/convert_element_type | solution.py:137
  (273 shorter events, 27.2 us)
Async XLA Ops:
  7.2 47.1 %copy-start = (bf16[256,1024]{1,0:T(8,128)(2,1)S(1)}, bf16[256,1024]{1,0:T(8,128)(2,1)}, u32[]{:S(2)}) copy-start(bf16[256,1024]{1,0:T(8,128)(2,1)} %param.19) | copy-start | bytes 1572868
  7.2 205.7 %reduce-scatter.2.cloned.1.call-start = ((), (), s32[]{:S(2)}) async-start(), calls=%async_computation.1 | async-start | bytes 2228224 | tf_op jit(solution)/shard_map/reduce_scatter | solution.py:84
  9.8 23.2 %copy-start.5 = (bf16[64,32,256]{2,1,0:T(8,128)(2,1)}, bf16[64,32,256]{2,1,0:T(8,128)(2,1)S(1)}, u32[]{:S(2)}) copy-start(bf16[64,32,256]{2,1,0:T(8,128)(2,1)S(1)} %broadcast_multiply_fusion) | copy-start | bytes 3145732
  9.8 1.4 collective-permute-start
  10.4 22.6 %copy-start.14 = (f32[64,32]{1,0:T(8,128)}, f32[64,32]{1,0:T(8,128)S(1)}, u32[]{:S(2)}) copy-start(f32[64,32]{1,0:T(8,128)S(1)} %copy.14) | copy-start | bytes 24580
  11.2 4.9 %collective-permute-start.1 = (bf16[3,32,256]{2,1,0:T(8,128)(2,1)S(1)}, bf16[3,32,256]{2,1,0:T(8,128)(2,1)S(1)}, u32[]{:S(2)}, u32[]{:S(2)}) collective-permute-start(bf16[3,32,256]{2,1,0:T(8,128)(2,1)S(1)} %collective-permute-done), channel_id=1, source_target_pairs={{0,2},{2,0},{1,3},{3,1},{4,6},{6,4},{5,7},{7,5},{8,10},{10,8},{9,1... | collective-permute-start | bytes 147464 | tf_op jit(solution)/shard_map/ppermute | solution.py:15
  16.1 4.1 %collective-permute-start.2 = (bf16[3,32,256]{2,1,0:T(8,128)(2,1)S(1)}, bf16[3,32,256]{2,1,0:T(8,128)(2,1)S(1)}, u32[]{:S(2)}, u32[]{:S(2)}) collective-permute-start(bf16[3,32,256]{2,1,0:T(8,128)(2,1)S(1)} %collective-permute-done.1), channel_id=1, source_target_pairs={{0,4},{4,0},{1,5},{5,1},{2,6},{6,2},{3,7},{7,3},{8,12},{12,8},{9,1... | collective-permute-start | bytes 147464 | tf_op jit(solution)/shard_map/ppermute | solution.py:15
  18.2 16.6 %copy-start.18 = (f32[1,1,256]{2,1,0:T(1,128)}, f32[1,1,256]{2,1,0:T(1,128)S(1)}, u32[]{:S(2)}) copy-start(f32[1,1,256]{2,1,0:T(1,128)S(1)} %get-tuple-element.113) | copy-start | bytes 3076
  18.2 16.6 %copy-start.20 = (f32[1,1,256]{2,1,0:T(1,128)}, f32[1,1,256]{2,1,0:T(1,128)S(1)}, u32[]{:S(2)}) copy-start(f32[1,1,256]{2,1,0:T(1,128)S(1)} %get-tuple-element.114) | copy-start | bytes 3076
  18.2 16.6 %copy-start.22 = (f32[1,1,256]{2,1,0:T(1,128)}, f32[1,1,256]{2,1,0:T(1,128)S(1)}, u32[]{:S(2)}) copy-start(f32[1,1,256]{2,1,0:T(1,128)S(1)} %get-tuple-element.115) | copy-start | bytes 3076
  18.2 16.6 %copy-start.24 = (f32[1,1,256]{2,1,0:T(1,128)}, f32[1,1,256]{2,1,0:T(1,128)S(1)}, u32[]{:S(2)}) copy-start(f32[1,1,256]{2,1,0:T(1,128)S(1)} %get-tuple-element.116) | copy-start | bytes 3076
  18.2 16.6 %copy-start.26 = (f32[1,1,256]{2,1,0:T(1,128)}, f32[1,1,256]{2,1,0:T(1,128)S(1)}, u32[]{:S(2)}) copy-start(f32[1,1,256]{2,1,0:T(1,128)S(1)} %get-tuple-element.117) | copy-start | bytes 3076
  18.3 16.6 %copy-start.28 = (f32[1,1,256]{2,1,0:T(1,128)}, f32[1,1,256]{2,1,0:T(1,128)S(1)}, u32[]{:S(2)}) copy-start(f32[1,1,256]{2,1,0:T(1,128)S(1)} %get-tuple-element.118) | copy-start | bytes 3076
  20.3 5.1 %collective-permute-start.3 = (bf16[3,32,256]{2,1,0:T(8,128)(2,1)S(1)}, bf16[3,32,256]{2,1,0:T(8,128)(2,1)S(1)}, u32[]{:S(2)}, u32[]{:S(2)}) collective-permute-start(bf16[3,32,256]{2,1,0:T(8,128)(2,1)S(1)} %collective-permute-done.2), channel_id=1, source_target_pairs={{0,8},{8,0},{1,9},{9,1},{2,10},{10,2},{3,11},{11,3},{4,12},{12,4},... | collective-permute-start | bytes 147464 | tf_op jit(solution)/shard_map/ppermute | solution.py:15
  25.6 7.4 %collective-permute-start.4 = (bf16[70,3,256]{2,1,0:T(4,128)(2,1)S(1)}, bf16[70,3,256]{2,1,0:T(4,128)(2,1)S(1)}, u32[]{:S(2)}, u32[]{:S(2)}) collective-permute-start(bf16[70,3,256]{2,1,0:T(4,128)(2,1)S(1)} %get-tuple-element.96), channel_id=1, source_target_pairs={{0,1},{1,2},{2,3},{3,4},{4,5},{5,6},{6,7},{7,8},{8,9},{9,10},{10,1... | collective-permute-start | bytes 322568 | tf_op jit(solution)/shard_map/ppermute | solution.py:25
  25.6 7.3 %collective-permute-start.5 = (bf16[70,3,256]{2,1,0:T(4,128)(2,1)S(1)}, bf16[70,3,256]{2,1,0:T(4,128)(2,1)S(1)}, u32[]{:S(2)}, u32[]{:S(2)}) collective-permute-start(bf16[70,3,256]{2,1,0:T(4,128)(2,1)S(1)} %get-tuple-element.97), channel_id=1, source_target_pairs={{1,0},{2,1},{3,2},{4,3},{5,4},{6,5},{7,6},{8,7},{9,8},{10,9},{11,1... | collective-permute-start | bytes 322568 | tf_op jit(solution)/shard_map/ppermute | solution.py:27
  79.5 22.6 %copy-start.3 = (f32[64,32,256]{2,1,0:T(8,128)}, f32[64,32,256]{2,1,0:T(8,128)S(1)}, u32[]{:S(2)}) copy-start(f32[64,32,256]{2,1,0:T(8,128)S(1)} %get-tuple-element.89) | copy-start | bytes 6291460
  79.8 26.9 %copy-start.8 = (bf16[64,32,256]{2,1,0:T(8,128)(2,1)S(1)}, bf16[64,32,256]{2,1,0:T(8,128)(2,1)}, u32[]{:S(2)}) copy-start(bf16[64,32,256]{2,1,0:T(8,128)(2,1)} %copy-done.7) | copy-start | bytes 3145732
  102.3 10.8 %collective-permute-start.6 = (bf16[70,3,256]{2,1,0:T(4,128)(2,1)S(1)}, bf16[70,3,256]{2,1,0:T(4,128)(2,1)S(1)}, u32[]{:S(2)}, u32[]{:S(2)}) collective-permute-start(bf16[70,3,256]{2,1,0:T(4,128)(2,1)S(1)} %get-tuple-element.94), channel_id=1, source_target_pairs={{0,1},{1,2},{2,3},{3,4},{4,5},{5,6},{6,7},{7,8},{8,9},{9,10},{10,1... | collective-permute-start | bytes 322568 | tf_op jit(solution)/shard_map/ppermute | solution.py:25
  103.0 10.1 %collective-permute-start.7 = (bf16[70,3,256]{2,1,0:T(4,128)(2,1)S(1)}, bf16[70,3,256]{2,1,0:T(4,128)(2,1)S(1)}, u32[]{:S(2)}, u32[]{:S(2)}) collective-permute-start(bf16[70,3,256]{2,1,0:T(4,128)(2,1)S(1)} %get-tuple-element.95), channel_id=1, source_target_pairs={{1,0},{2,1},{3,2},{4,3},{5,4},{6,5},{7,6},{8,7},{9,8},{10,9},{11,1... | collective-permute-start | bytes 322568 | tf_op jit(solution)/shard_map/ppermute | solution.py:27
  128.2 3.2 %collective-permute-start.8 = (bf16[3,32,256]{2,1,0:T(8,128)(2,1)S(1)}, bf16[3,32,256]{2,1,0:T(8,128)(2,1)}, u32[]{:S(2)}, u32[]{:S(2)}) collective-permute-start(bf16[3,32,256]{2,1,0:T(8,128)(2,1)S(1)} %slice.1409), channel_id=1, source_target_pairs={{0,1},{1,0},{2,3},{3,2},{4,5},{5,4},{6,7},{7,6},{8,9},{9,8},{10,11... | collective-permute-start | bytes 147464 | tf_op jit(solution)/shard_map/ppermute | solution.py:15
  131.5 6.4 %collective-permute-start.9 = (bf16[3,32,256]{2,1,0:T(8,128)(2,1)}, bf16[3,32,256]{2,1,0:T(8,128)(2,1)}, u32[]{:S(2)}, u32[]{:S(2)}) collective-permute-start(bf16[3,32,256]{2,1,0:T(8,128)(2,1)} %collective-permute-done.8), channel_id=1, source_target_pairs={{0,2},{2,0},{1,3},{3,1},{4,6},{6,4},{5,7},{7,5},{8,10},{10,8},{9,1... | collective-permute-start | bytes 147464 | tf_op jit(solution)/shard_map/ppermute | solution.py:15
  137.9 6.1 %collective-permute-start.10 = (bf16[3,32,256]{2,1,0:T(8,128)(2,1)}, bf16[3,32,256]{2,1,0:T(8,128)(2,1)}, u32[]{:S(2)}, u32[]{:S(2)}) collective-permute-start(bf16[3,32,256]{2,1,0:T(8,128)(2,1)} %collective-permute-done.9), channel_id=1, source_target_pairs={{0,4},{4,0},{1,5},{5,1},{2,6},{6,2},{3,7},{7,3},{8,12},{12,8},{9,1... | collective-permute-start | bytes 147464 | tf_op jit(solution)/shard_map/ppermute | solution.py:15
  144.0 65.4 %collective-permute-start.11 = (bf16[3,32,256]{2,1,0:T(8,128)(2,1)}, bf16[3,32,256]{2,1,0:T(8,128)(2,1)S(1)}, u32[]{:S(2)}, u32[]{:S(2)}) collective-permute-start(bf16[3,32,256]{2,1,0:T(8,128)(2,1)} %collective-permute-done.10), channel_id=1, source_target_pairs={{0,8},{8,0},{1,9},{9,1},{2,10},{10,2},{3,11},{11,3},{4,12},{12,4},... | collective-permute-start | bytes 147464 | tf_op jit(solution)/shard_map/ppermute | solution.py:15
  (100 other events, 601.3 us)
Sparse Core Ops, SparseCore 0:
  131.6 59.5 reduce-scatter.1
where the time goes:
time: 222 us; the launch traced here: 221 us
  other arithmetic  76.8 us (35%)
  blocking collectives  61.8 us (28%)
  local copies, waits for them, and re-layouts  21.1 us (10%)
  starting transfers between devices  19.4 us (9%)
  matrix products  18.8 us (8%)
  between operations  15.8 us (7%)
  waiting for transfers between devices  7.55 us (3%)
    psum x1, blocking collectives, local(): grad_kernel = lax.psum(local_kernel, 'lon')  61.8 us
    another operation x1, other arithmetic  22.2 us
    reduce_sum x3, other arithmetic, local(): jnp.sum(grad_conv * ext_wide[row_tap:row_tap + band_rows, col_tap:col_tap...  17.1 us
    reduce_sum x1, other arithmetic, local(): mean_z = jnp.mean(conv, axis=-1, keepdims=True)  15.9 us
    ppermute x8, starting transfers between devices, from_partner(): return lax.ppermute(block, axis, route)  10.4 us
    ppermute x2, starting transfers between devices, extended_2(): lax.ppermute(head, axis, [((i + 1) % count, i) for i in range(count)])  8.19 us
    dot_general x1, matrix products, local(): dhid = jnp.dot(dout, down_weight, preferred_element_type=jnp.float32)  6.25 us
    scatter-add x1, local copies, waits for them, and re-layouts, local(): grad_padded = grad_padded.at[:, :3].add(arrived[:, :3])  5.24 us
  transfers between devices with their start and end apart: 13, of which 5 were waited for; matrix products, arithmetic and copies ran while one was open for 13% of the time, Pallas kernels for 0%

commit v1 on v0

--- a/solution.py
+++ b/solution.py
@@ -107,7 +107,7 @@
                 )
             )
     local_kernel = jnp.stack(taps, axis=0).reshape(7, 7, channels) * factor
-    grad_kernel = lax.psum(local_kernel, "lon")
+    grad_kernel = jnp.sum(lax.all_gather(local_kernel, "lon"), axis=0)
     grad_pad = jnp.pad(grad_conv, ((6, 6), (6, 6), (0, 0)))
     grad_ext = jnp.zeros((band_rows + 6, band_cols + 6, channels), jnp.float32)
     for row_tap in range(7):

time: 222 us -> 190 us (0.86)
  blocking collectives: 61.8 us -> 23.7 us
  waiting for transfers between devices: 7.55 us -> 13.6 us
  other arithmetic: 76.8 us -> 79.5 us
  matrix products: 18.8 us -> 16.5 us
    psum x1 -> x0, blocking collectives: 61.8 us -> none  [local(): grad_kernel = lax.psum(local_kernel, 'lon')]
    all_gather x0 -> x1, blocking collectives: none -> 23.7 us  [local(): grad_kernel = jnp.sum(lax.all_gather(local_kernel, 'lon'), axis=0)]
    ppermute x8, waiting for transfers between devices: 4.87 us -> 10.9 us  [from_partner(): return lax.ppermute(block, axis, route)]
    dot_general x1, matrix products: 4.53 us -> 2.26 us  [local(): lax.dot_general(normed, dpre, contract_rows, preferred_element_type=jnp.f...]
  transfers between devices with their start and end apart: 13 -> 13, of which waited for: 5 -> 6; matrix products, arithmetic and copies ran while one was open for 13% -> 22% of each run, Pallas kernels for 0% -> 0%
where the time goes in v1:
time: 190 us; the launch traced here: 189 us
  other arithmetic  79.5 us (42%)
  blocking collectives  23.7 us (12%)
  local copies, waits for them, and re-layouts  21.9 us (12%)
  starting transfers between devices  18.4 us (10%)
  matrix products  16.5 us (9%)
  between operations  15.7 us (8%)
  waiting for transfers between devices  13.6 us (7%)
    all_gather x1, blocking collectives, local(): grad_kernel = jnp.sum(lax.all_gather(local_kernel, 'lon'), axis=0)  23.7 us
    another operation x1, other arithmetic  22.8 us
    reduce_sum x3, other arithmetic, local(): jnp.sum(grad_conv * ext_wide[row_tap:row_tap + band_rows, col_tap:col_tap...  17.2 us
    reduce_sum x1, other arithmetic, local(): mean_z = jnp.mean(conv, axis=-1, keepdims=True)  16.1 us
    ppermute x8, waiting for transfers between devices, from_partner(): return lax.ppermute(block, axis, route)  10.9 us
    ppermute x8, starting transfers between devices, from_partner(): return lax.ppermute(block, axis, route)  9.39 us
    ppermute x2, starting transfers between devices, extended_2(): lax.ppermute(head, axis, [((i + 1) % count, i) for i in range(count)])  8.19 us
    dot_general x1, matrix products, local(): dhid = jnp.dot(dout, down_weight, preferred_element_type=jnp.float32)  6.25 us
  transfers between devices with their start and end apart: 13, of which 6 were waited for; matrix products, arithmetic and copies ran while one was open for 22% of the time, Pallas kernels for 0%

profile of v1, /device:TPU:0, one launch (start us, length us, event | category | flops | bytes accessed | tf_op | source)
XLA Modules:
  0.0 189.4 jit_solution(9124217590220330203)
XLA Ops:
  11.2 2.9 %collective-permute-start.1 = (bf16[3,32,256]{2,1,0:T(8,128)(2,1)S(1)}, bf16[3,32,256]{2,1,0:T(8,128)(2,1)S(1)}, u32[]{:S(2)}, u32[]{:S(2)}) collective-permute-start(bf16[3,32,256]{2,1,0:T(8,128)(2,1)S(1)} %collective-permute-done), channel_id=1, source_target_pairs={{0,2},{2,0},{1,3},{3,1},{4,6},{6,4},{5,7},{7,5},{8,10},{10,8},{9,1... | collective-permute-start | bytes 147464 | tf_op jit(solution)/shard_map/ppermute | solution.py:15
  20.3 3.0 %collective-permute-start.3 = (bf16[3,32,256]{2,1,0:T(8,128)(2,1)S(1)}, bf16[3,32,256]{2,1,0:T(8,128)(2,1)S(1)}, u32[]{:S(2)}, u32[]{:S(2)}) collective-permute-start(bf16[3,32,256]{2,1,0:T(8,128)(2,1)S(1)} %collective-permute-done.2), channel_id=1, source_target_pairs={{0,8},{8,0},{1,9},{9,1},{2,10},{10,2},{3,11},{11,3},{4,12},{12,4},... | collective-permute-start | bytes 147464 | tf_op jit(solution)/shard_map/ppermute | solution.py:15
  25.6 4.4 %collective-permute-start.5 = (bf16[70,3,256]{2,1,0:T(4,128)(2,1)S(1)}, bf16[70,3,256]{2,1,0:T(4,128)(2,1)S(1)}, u32[]{:S(2)}, u32[]{:S(2)}) collective-permute-start(bf16[70,3,256]{2,1,0:T(4,128)(2,1)S(1)} %get-tuple-element.97), channel_id=1, source_target_pairs={{1,0},{2,1},{3,2},{4,3},{5,4},{6,5},{7,6},{8,7},{9,8},{10,9},{11,1... | collective-permute-start | bytes 322568 | tf_op jit(solution)/shard_map/ppermute | solution.py:27
  30.3 2.7 %collective-permute-done.4 = bf16[70,3,256]{2,1,0:T(4,128)(2,1)S(1)} collective-permute-done((bf16[70,3,256]{2,1,0:T(4,128)(2,1)S(1)}, bf16[70,3,256]{2,1,0:T(4,128)(2,1)S(1)}, u32[]{:S(2)}, u32[]{:S(2)}) %collective-permute-start.4) | collective-permute-done | bytes 107552 | tf_op jit(solution)/shard_map/ppermute | solution.py:25
  35.2 16.1 %fusion.115 = (f32[64,32]{1,0:T(8,128)S(1)}, f32[64,32,256]{2,1,0:T(8,128)}) fusion(f32[70,38,256]{2,1,0:T(8,128)S(1)} %maximum_convert_fusion, f32[256]{0:T(256)S(1)} %bitcast.211, f32[256]{0:T(256)S(1)} %bitcast.213, f32[256]{0:T(256)S(1)} %bitcast.119, f32[256]{0:T(256)S(1)} %bitcast.121, f32[256]{0:T(256)S(1)} %bitcast.123, f32[256]{0:T(256)S(1)} %bitcast.125, ...), kind=kLoop, calls=%fused_computation.242 | loop fusion | flops 51378176 | bytes 104915968 | tf_op jit(solution)/shard_map/reduce_sum | solution.py:62
  51.3 2.4 %multiply_reduce_fusion.51 = f32[64,32]{1,0:T(8,128)S(1)} fusion(f32[64,32,256]{2,1,0:T(8,128)} %get-tuple-element.93, f32[64,32]{1,0:T(8,128)S(1)} %broadcast_multiply_fusion.3), kind=kLoop, calls=%fused_computation.216 | loop fusion | flops 1570816 | bytes 2113536 | tf_op jit(solution)/shard_map/reduce_sum | solution.py:64
  55.7 4.2 %fusion.7 = f32[256,1024]{1,0:T(8,128)} fusion(bf16[2048,256]{1,0:T(8,128)(2,1)S(1)} %bitcast.115, f32[2048,1024]{1,0:T(8,128)S(1)} %fusion.121), kind=kOutput, calls=%fused_computation.59 | convolution fusion | flops 1092616192 | bytes 10485760 | tf_op jit(solution)/shard_map/dot_general | solution.py:83
  59.9 6.3 %fusion.6 = bf16[2048,1024]{1,0:T(8,128)(2,1)S(1)} fusion(f32[2048,1024]{1,0:T(8,128)S(1)} %fusion.121, bf16[2048,256]{1,0:T(8,128)(2,1)S(1)} %bitcast.116, bf16[256,1024]{1,0:T(8,128)(2,1)S(1)} %copy-done.107), kind=kOutput, calls=%fused_computation.57 | convolution fusion | flops 1115684864 | bytes 14155776 | tf_op jit(solution)/shard_map/dot_general | solution.py:75
  66.2 2.3 %fusion.122 = f32[256,1024]{1,0:T(8,128)} fusion(bf16[2048,256]{1,0:T(8,128)(2,1)S(1)} %bitcast.114, bf16[2048,1024]{1,0:T(8,128)(2,1)S(1)} %fusion.6), kind=kOutput, calls=%fused_computation.249 | convolution fusion | flops 1073741824 | bytes 6291456 | tf_op jit(solution)/shard_map/dot_general | solution.py:82
  68.4 2.6 %multiply_reduce_fusion.50 = (f32[2048]{0:T(1024)S(1)}, f32[2048,256]{1,0:T(8,128)}) fusion(f32[256]{0:T(256)S(1)} %copy-done.15, bf16[2048,1024]{1,0:T(8,128)(2,1)S(1)} %fusion.6, bf16[256,1024]{1,0:T(8,128)(2,1)S(1)} %copy-done), kind=kOutput, calls=%fused_computation.214 | convolution fusion | flops 1074788352 | bytes 6824960 | tf_op jit(solution)/shard_map/dot_general | solution.py:92
  71.1 2.9 %multiply_reduce_fusion.49 = f32[64,32]{1,0:T(8,128)S(1)} fusion(f32[64,32,256]{2,1,0:T(8,128)} %bitcast.112, f32[64,32,256]{2,1,0:T(8,128)} %get-tuple-element.93, f32[256]{0:T(256)S(1)} %copy-done.15, f32[64,32]{1,0:T(8,128)S(1)} %add_rsqrt_fusion, f32[64,32]{1,0:T(8,128)S(1)} %broadcast_multiply_fusion.3), kind=kLoop, calls=%fused_computation.213 | loop fusion | flops 2619392 | bytes 4219904 | tf_op jit(solution)/shard_map/reduce_sum | solution.py:97
  74.9 6.7 %multiply_reduce_fusion = (f32[256]{0:T(256)}, f32[256]{0:T(256)}, f32[256]{0:T(256)}, f32[256]{0:T(256)}, f32[256]{0:T(256)}, /*index=5*/f32[256]{0:T(256)}, f3...) fusion(f32[70,38,256]{2,1,0:T(8,128)S(1)} %maximum_convert_fusi, ...), kind=kLoop, calls=%fused_computation.163 | loop fusion | flops 22539776 | bytes 44092416 | tf_op jit(solution)/shard_map/reduce_sum | solution.py:103
  82.0 22.8 %fusion.113 = (bf16[70,38,256]{2,1,0:T(8,128)(2,1)S(1)}, f32[70,38,256]{2,1,0:T(8,128)}) fusion(f32[256]{0:T(256)S(1)} %bitcast.212, f32[256]{0:T(256)S(1)} %bitcast.214, f32[256]{0:T(256)S(1)} %bitcast.120, f32[256]{0:T(256)S(1)} %bitcast.122, f32[256]{0:T(256)S(1)} %bitcast.124, f32[256]{0:T(256)S(1)} %bitcast.126, f32[256]{0:T(256)S(1)} %bitcast.128, ...), kind=kLoop, calls=%fused_computation.241 | loop fusion | flops 66734080 | bytes 6233088 | tf_op jit(solution)/shard_map/convert.3
  106.2 3.8 %collective-permute-start.7 = (bf16[70,3,256]{2,1,0:T(4,128)(2,1)}, bf16[70,3,256]{2,1,0:T(4,128)(2,1)}, u32[]{:S(2)}, u32[]{:S(2)}) collective-permute-start(bf16[70,3,256]{2,1,0:T(4,128)(2,1)} %get-tuple-element.95), channel_id=1, source_target_pairs={{1,0},{2,1},{3,2},{4,3},{5,4},{6,5},{7,6},{8,7},{9,8},{10,9},{11,1... | collective-permute-start | bytes 322568 | tf_op jit(solution)/shard_map/ppermute | solution.py:27
  111.6 3.6 %slice.866 = f32[70,32,256]{2,1,0:T(8,128)} slice(f32[70,38,256]{2,1,0:T(8,128)} %get-tuple-element.91), slice={[0:70], [3:35], [0:256]} | slice | bytes 4587520 | tf_op jit(solution)/shard_map/slice | solution.py:124
  115.2 2.2 %convert_add_fusion.1 = f32[70,3,256]{2,1,0:T(4,128)} fusion(f32[70,38,256]{2,1,0:T(8,128)} %get-tuple-element.91, bf16[70,3,256]{2,1,0:T(4,128)(2,1)} %collective-permute-done.7, bf16[70,3,256]{2,1,0:T(4,128)(2,1)S(1)} %get-tuple-element.94, bf16[70,3,256]{2,1,0:T(4,128)(2,1)} %get-tuple-element.95, bf16[70,3,256]{2,1,0:T(4,128)(2,1)} %collective-permute-done.6), kind=kLoop, calls=%fused_computation.222 | loop fusion | flops 483840 | bytes 860160 | tf_op jit(solution)/shard_map/add | solution.py:125
  117.5 5.3 %scatter-add.10 = f32[70,32,256]{2,1,0:T(8,128)} dynamic-update-slice(f32[70,32,256]{2,1,0:T(8,128)} %slice.866, f32[70,3,256]{2,1,0:T(4,128)} %convert_add_fusion.1, s32[]{:T(128)} %constant.108.clone.1, s32[]{:T(128)} %constant.108.clone.1, s32[]{:T(128)} %constant.108.clone.1) | dynamic-update-slice | bytes 430084 | tf_op jit(solution)/shard_map/scatter-add | solution.py:125
  122.7 2.2 %slice_add_fusion = f32[70,3,256]{2,1,0:T(4,128)} fusion(f32[70,32,256]{2,1,0:T(8,128)} %scatter-add.10, bf16[70,3,256]{2,1,0:T(4,128)(2,1)} %collective-permute-done.7, bf16[70,3,256]{2,1,0:T(4,128)(2,1)S(1)} %get-tuple-element.94, bf16[70,3,256]{2,1,0:T(4,128)(2,1)} %get-tuple-element.95, bf16[70,3,256]{2,1,0:T(4,128)(2,1)} %collective-permute-done.6), kind=kLoop, calls=%fused_computation.221 | loop fusion | flops 483840 | bytes 860160 | tf_op jit(solution)/shard_map/add | solution.py:126
  124.9 4.6 %scatter-add.11 = f32[70,32,256]{2,1,0:T(8,128)} dynamic-update-slice(f32[70,32,256]{2,1,0:T(8,128)} %scatter-add.10, f32[70,3,256]{2,1,0:T(4,128)} %slice_add_fusion, s32[]{:T(128)} %constant.108.clone.1, s32[]{:T(128)} %constant.109.clone.1, s32[]{:T(128)} %constant.108.clone.1) | dynamic-update-slice | bytes 430084 | tf_op jit(solution)/shard_map/scatter-add | solution.py:126
  130.5 6.1 %multiply_reduce_fusion.18 = (f32[256]{0:T(256)S(1)}, f32[256]{0:T(256)S(1)}, f32[256]{0:T(256)S(1)}, f32[256]{0:T(256)S(1)}, f32[256]{0:T(256)S(1)}, /*index=5*...) fusion(f32[64,32,256]{2,1,0:T(8,128)} %copy-done.3, ...), kind=kLoop, calls=%fused_computation.181 | loop fusion | flops 18869760 | bytes 39864320 | tf_op jit(solution)/shard_map/reduce_sum | solution.py:103
  136.9 4.3 %multiply_reduce_fusion.36 = (f32[256]{0:T(256)S(1)}, f32[256]{0:T(256)S(1)}, f32[256]{0:T(256)S(1)}, f32[256]{0:T(256)S(1)}, f32[256]{0:T(256)}, /*index=5*/f32...) fusion(f32[64,32,256]{2,1,0:T(8,128)S(1)} %copy-done.4, ...), kind=kLoop, calls=%fused_computation.199 | loop fusion | flops 13628160 | bytes 29373440 | tf_op jit(solution)/shard_map/reduce_sum | solution.py:103
  143.2 6.0 %collective-permute-done.10 = bf16[3,32,256]{2,1,0:T(8,128)(2,1)S(1)} collective-permute-done((bf16[3,32,256]{2,1,0:T(8,128)(2,1)}, bf16[3,32,256]{2,1,0:T(8,128)(2,1)S(1)}, u32[]{:S(2)}, u32[]{:S(2)}) %collective-permute-start.10) | collective-permute-done | bytes 49184 | tf_op jit(solution)/shard_map/ppermute | solution.py:15
  149.9 23.7 %all_gather.4 = f32[16,7,7,256]{3,2,1,0:T(8,128)} all-gather(f32[1,7,7,256]{3,2,1,0:T(8,128)S(1)} %mul.1504), channel_id=1, replica_groups=mesh['groups'=2,'lon'=16] {'lon'}, dimensions={0}, use_global_device_ids=true | all-gather | bytes 852992 | tf_op jit(solution)/shard_map/all_gather | solution.py:110
  177.8 3.2 %fusion.107 = bf16[64,32,256]{2,1,0:T(8,128)(2,1)} fusion(bf16[64,32,256]{2,1,0:T(8,128)(2,1)} %param.16, f32[64,32,256]{2,1,0:T(8,128)} %fusion.108, f32[64,32]{1,0:T(8,128)S(1)} %copy-done.13), kind=kLoop, calls=%fused_computation.161 | loop fusion | flops 2097152 | bytes 4202496 | tf_op jit(solution)/shard_map/convert_element_type | solution.py:137
  (268 shorter events, 29.5 us)
Async XLA Ops:
  7.2 47.3 %copy-start = (bf16[256,1024]{1,0:T(8,128)(2,1)S(1)}, bf16[256,1024]{1,0:T(8,128)(2,1)}, u32[]{:S(2)}) copy-start(bf16[256,1024]{1,0:T(8,128)(2,1)} %param.19) | copy-start | bytes 1572868
  7.2 173.8 %reduce-scatter.2.cloned.1.call-start = ((), (), s32[]{:S(2)}) async-start(), calls=%async_computation.1 | async-start | bytes 2228224 | tf_op jit(solution)/shard_map/reduce_scatter | solution.py:84
  9.8 23.2 %copy-start.6 = (bf16[64,32,256]{2,1,0:T(8,128)(2,1)}, bf16[64,32,256]{2,1,0:T(8,128)(2,1)S(1)}, u32[]{:S(2)}) copy-start(bf16[64,32,256]{2,1,0:T(8,128)(2,1)S(1)} %broadcast_multiply_fusion) | copy-start | bytes 3145732
  9.8 1.4 collective-permute-start
  10.4 22.6 %copy-start.12 = (f32[64,32]{1,0:T(8,128)}, f32[64,32]{1,0:T(8,128)S(1)}, u32[]{:S(2)}) copy-start(f32[64,32]{1,0:T(8,128)S(1)} %copy.16) | copy-start | bytes 24580
  11.2 4.9 %collective-permute-start.1 = (bf16[3,32,256]{2,1,0:T(8,128)(2,1)S(1)}, bf16[3,32,256]{2,1,0:T(8,128)(2,1)S(1)}, u32[]{:S(2)}, u32[]{:S(2)}) collective-permute-start(bf16[3,32,256]{2,1,0:T(8,128)(2,1)S(1)} %collective-permute-done), channel_id=1, source_target_pairs={{0,2},{2,0},{1,3},{3,1},{4,6},{6,4},{5,7},{7,5},{8,10},{10,8},{9,1... | collective-permute-start | bytes 147464 | tf_op jit(solution)/shard_map/ppermute | solution.py:15
  16.1 4.1 %collective-permute-start.2 = (bf16[3,32,256]{2,1,0:T(8,128)(2,1)S(1)}, bf16[3,32,256]{2,1,0:T(8,128)(2,1)S(1)}, u32[]{:S(2)}, u32[]{:S(2)}) collective-permute-start(bf16[3,32,256]{2,1,0:T(8,128)(2,1)S(1)} %collective-permute-done.1), channel_id=1, source_target_pairs={{0,4},{4,0},{1,5},{5,1},{2,6},{6,2},{3,7},{7,3},{8,12},{12,8},{9,1... | collective-permute-start | bytes 147464 | tf_op jit(solution)/shard_map/ppermute | solution.py:15
  18.2 16.6 %copy-start.16 = (f32[1,1,256]{2,1,0:T(1,128)}, f32[1,1,256]{2,1,0:T(1,128)S(1)}, u32[]{:S(2)}) copy-start(f32[1,1,256]{2,1,0:T(1,128)S(1)} %get-tuple-element.113) | copy-start | bytes 3076
  18.2 16.6 %copy-start.18 = (f32[1,1,256]{2,1,0:T(1,128)}, f32[1,1,256]{2,1,0:T(1,128)S(1)}, u32[]{:S(2)}) copy-start(f32[1,1,256]{2,1,0:T(1,128)S(1)} %get-tuple-element.114) | copy-start | bytes 3076
  18.2 16.6 %copy-start.20 = (f32[1,1,256]{2,1,0:T(1,128)}, f32[1,1,256]{2,1,0:T(1,128)S(1)}, u32[]{:S(2)}) copy-start(f32[1,1,256]{2,1,0:T(1,128)S(1)} %get-tuple-element.115) | copy-start | bytes 3076
  18.2 16.6 %copy-start.22 = (f32[1,1,256]{2,1,0:T(1,128)}, f32[1,1,256]{2,1,0:T(1,128)S(1)}, u32[]{:S(2)}) copy-start(f32[1,1,256]{2,1,0:T(1,128)S(1)} %get-tuple-element.116) | copy-start | bytes 3076
  20.3 5.1 %collective-permute-start.3 = (bf16[3,32,256]{2,1,0:T(8,128)(2,1)S(1)}, bf16[3,32,256]{2,1,0:T(8,128)(2,1)S(1)}, u32[]{:S(2)}, u32[]{:S(2)}) collective-permute-start(bf16[3,32,256]{2,1,0:T(8,128)(2,1)S(1)} %collective-permute-done.2), channel_id=1, source_target_pairs={{0,8},{8,0},{1,9},{9,1},{2,10},{10,2},{3,11},{11,3},{4,12},{12,4},... | collective-permute-start | bytes 147464 | tf_op jit(solution)/shard_map/ppermute | solution.py:15
  25.6 7.4 %collective-permute-start.4 = (bf16[70,3,256]{2,1,0:T(4,128)(2,1)S(1)}, bf16[70,3,256]{2,1,0:T(4,128)(2,1)S(1)}, u32[]{:S(2)}, u32[]{:S(2)}) collective-permute-start(bf16[70,3,256]{2,1,0:T(4,128)(2,1)S(1)} %get-tuple-element.96), channel_id=1, source_target_pairs={{0,1},{1,2},{2,3},{3,4},{4,5},{5,6},{6,7},{7,8},{8,9},{9,10},{10,1... | collective-permute-start | bytes 322568 | tf_op jit(solution)/shard_map/ppermute | solution.py:25
  25.6 7.3 %collective-permute-start.5 = (bf16[70,3,256]{2,1,0:T(4,128)(2,1)S(1)}, bf16[70,3,256]{2,1,0:T(4,128)(2,1)S(1)}, u32[]{:S(2)}, u32[]{:S(2)}) collective-permute-start(bf16[70,3,256]{2,1,0:T(4,128)(2,1)S(1)} %get-tuple-element.97), channel_id=1, source_target_pairs={{1,0},{2,1},{3,2},{4,3},{5,4},{6,5},{7,6},{8,7},{9,8},{10,9},{11,1... | collective-permute-start | bytes 322568 | tf_op jit(solution)/shard_map/ppermute | solution.py:27
  81.6 23.2 %copy-start.3 = (f32[64,32,256]{2,1,0:T(8,128)}, f32[64,32,256]{2,1,0:T(8,128)S(1)}, u32[]{:S(2)}) copy-start(f32[64,32,256]{2,1,0:T(8,128)S(1)} %get-tuple-element.89) | copy-start | bytes 6291460
  82.0 28.1 %copy-start.10 = (f32[256,1024]{1,0:T(8,128)S(1)}, f32[256,1024]{1,0:T(8,128)}, u32[]{:S(2)}) copy-start(f32[256,1024]{1,0:T(8,128)} %fusion.7) | copy-start | bytes 3145732
  82.0 28.0 %copy-start.11 = (f32[256,1024]{1,0:T(8,128)S(1)}, f32[256,1024]{1,0:T(8,128)}, u32[]{:S(2)}) copy-start(f32[256,1024]{1,0:T(8,128)} %fusion.122) | copy-start | bytes 3145732
  105.6 9.6 %collective-permute-start.6 = (bf16[70,3,256]{2,1,0:T(4,128)(2,1)S(1)}, bf16[70,3,256]{2,1,0:T(4,128)(2,1)}, u32[]{:S(2)}, u32[]{:S(2)}) collective-permute-start(bf16[70,3,256]{2,1,0:T(4,128)(2,1)S(1)} %get-tuple-element.94), channel_id=1, source_target_pairs={{0,1},{1,2},{2,3},{3,4},{4,5},{5,6},{6,7},{7,8},{8,9},{9,10},{10,1... | collective-permute-start | bytes 322568 | tf_op jit(solution)/shard_map/ppermute | solution.py:25
  106.2 9.0 %collective-permute-start.7 = (bf16[70,3,256]{2,1,0:T(4,128)(2,1)}, bf16[70,3,256]{2,1,0:T(4,128)(2,1)}, u32[]{:S(2)}, u32[]{:S(2)}) collective-permute-start(bf16[70,3,256]{2,1,0:T(4,128)(2,1)} %get-tuple-element.95), channel_id=1, source_target_pairs={{1,0},{2,1},{3,2},{4,3},{5,4},{6,5},{7,6},{8,7},{9,8},{10,9},{11,1... | collective-permute-start | bytes 322568 | tf_op jit(solution)/shard_map/ppermute | solution.py:27
  130.4 6.4 %collective-permute-start.8 = (bf16[3,32,256]{2,1,0:T(8,128)(2,1)S(1)}, bf16[3,32,256]{2,1,0:T(8,128)(2,1)}, u32[]{:S(2)}, u32[]{:S(2)}) collective-permute-start(bf16[3,32,256]{2,1,0:T(8,128)(2,1)S(1)} %slice.1409), channel_id=1, source_target_pairs={{0,1},{1,0},{2,3},{3,2},{4,5},{5,4},{6,7},{7,6},{8,9},{9,8},{10,11... | collective-permute-start | bytes 147464 | tf_op jit(solution)/shard_map/ppermute | solution.py:15
  136.8 6.3 %collective-permute-start.9 = (bf16[3,32,256]{2,1,0:T(8,128)(2,1)}, bf16[3,32,256]{2,1,0:T(8,128)(2,1)}, u32[]{:S(2)}, u32[]{:S(2)}) collective-permute-start(bf16[3,32,256]{2,1,0:T(8,128)(2,1)} %collective-permute-done.8), channel_id=1, source_target_pairs={{0,2},{2,0},{1,3},{3,1},{4,6},{6,4},{5,7},{7,5},{8,10},{10,8},{9,1... | collective-permute-start | bytes 147464 | tf_op jit(solution)/shard_map/ppermute | solution.py:15
  141.2 34.3 %copy-start.5 = (f32[70,32,256]{2,1,0:T(8,128)S(1)}, f32[70,32,256]{2,1,0:T(8,128)}, u32[]{:S(2)}) copy-start(f32[70,32,256]{2,1,0:T(8,128)} %scatter-add.11) | copy-start | bytes 6881284
  143.1 6.2 %collective-permute-start.10 = (bf16[3,32,256]{2,1,0:T(8,128)(2,1)}, bf16[3,32,256]{2,1,0:T(8,128)(2,1)S(1)}, u32[]{:S(2)}, u32[]{:S(2)}) collective-permute-start(bf16[3,32,256]{2,1,0:T(8,128)(2,1)} %collective-permute-done.9), channel_id=1, source_target_pairs={{0,4},{4,0},{1,5},{5,1},{2,6},{6,2},{3,7},{7,3},{8,12},{12,8},{9,1... | collective-permute-start | bytes 147464 | tf_op jit(solution)/shard_map/ppermute | solution.py:15
  149.2 27.8 %collective-permute-start.11 = (bf16[3,32,256]{2,1,0:T(8,128)(2,1)S(1)}, bf16[3,32,256]{2,1,0:T(8,128)(2,1)S(1)}, u32[]{:S(2)}, u32[]{:S(2)}) collective-permute-start(bf16[3,32,256]{2,1,0:T(8,128)(2,1)S(1)} %collective-permute-done.10), channel_id=1, source_target_pairs={{0,8},{8,0},{1,9},{9,1},{2,10},{10,2},{3,11},{11,3},{4,12},{12,4},... | collective-permute-start | bytes 147464 | tf_op jit(solution)/shard_map/ppermute | solution.py:15
  (97 other events, 620.9 us)
Sparse Core Ops, SparseCore 0:
  111.7 60.6 reduce-scatter.1
